TPU v7x, 256 devices: a whole 4x4x8 slice. The times are simulated.
256 devices in a mesh: row: 8 (over z_hi, x), col: 32 (over z_lo, y, core).
Axes of the slice: x: 4, y: 4, z: 8 (z_hi: 2, z_lo: 4; z = z_hi * 4 + z_lo), core: 2. Of those that a mesh axis runs over, the one named last changes fastest.
Arguments:
- contexts: bfloat16 [32768, 128], P(('row', 'col')), may hold values from -8 to 8
- logged_actions: int32 [32768], P(('row', 'col')), may hold values from 0 to 131041
- policy_actions: int32 [32768, 8], P(('row', 'col')), may hold values from 0 to 131041
- rewards: float32 [32768], P(('row', 'col')), may hold values from 0.2 to 2
Outputs:
- weights: float32 [32768, 8], P(('row', 'col'))
- residual: float32 [32768, 8], P(('row', 'col'))
- values: float32 [8], replicated
All inputs are finite; a program needn't handle non-finite values.
Results may differ from a plain program's by a relative error of at most 0.0056.
Values may be sent and summed in bfloat16 or wider, within the bound.
No kernel may reach another device: no remote copies, remote signals or barrier semaphores. Data moves between devices by JAX's collectives and lax.ppermute only.
A program may use at most 64 MiB of HBM per device.

v0:
```python
import math
import jax
import jax.numpy as jnp
from jax import lax
from jax.sharding import PartitionSpec as P

NPOL = 8
NACT = 16
CATALOG = 131042
ridge = 0.1
group_size = 16
stride_base = 1009
phase_step = 0.37
two_pi = 2.0 * math.pi


def action_features(chosen, width):
    levels = jnp.arange(width, dtype=jnp.int32)
    multipliers = 1 + stride_base * levels
    turned = chosen[..., None] * multipliers % CATALOG
    angles = turned.astype(jnp.float32) * (two_pi / CATALOG) + phase_step * levels.astype(
        jnp.float32
    )
    wave_terms = math.sqrt(2.0 / width) * jnp.cos(angles)
    constant_term = jnp.full(wave_terms.shape, 1.0 / math.sqrt(width), jnp.float32)
    return jnp.where(levels == 0, constant_term, wave_terms).astype(jnp.bfloat16)


def select_actions(products, onehot):
    shaped = products.reshape(
        products.shape[:-1] + (products.shape[-1] // onehot.shape[-1], onehot.shape[-1])
    )
    return jnp.sum(shaped * jnp.expand_dims(onehot.astype(jnp.float32), -2), axis=-1)


def kernel_tiles(left_tiles, right_tiles, left_squares, right_squares):
    inner = jnp.einsum("grd,gsd->grs", left_tiles, right_tiles, preferred_element_type=jnp.float32)
    expo = (2.0 * inner - left_squares[:, :, None] - right_squares[:, None, :]) / left_tiles.shape[
        -1
    ]
    return jnp.exp(expo).astype(jnp.bfloat16)


def tile_terms(kernel, left_matrix, right_matrix, left_onehot, right_onehot):
    toward_left = jnp.einsum(
        "grs,gsm->grm", kernel, right_matrix, preferred_element_type=jnp.float32
    )
    toward_right = jnp.einsum(
        "grs,grm->gsm", kernel, left_matrix, preferred_element_type=jnp.float32
    )
    return (select_actions(toward_left, left_onehot), select_actions(toward_right, right_onehot))


def listed_pass(
    left_ctx,
    left_squares,
    left_matrix,
    left_onehot,
    right_ctx,
    right_squares,
    right_matrix,
    right_onehot,
    placed,
    diagonal,
):
    left_count = left_ctx.shape[0]
    tile_rows = left_ctx.shape[1]
    right_count = right_ctx.shape[0]
    policies = left_matrix.shape[-1] // left_onehot.shape[-1]
    flat_placed = placed.reshape(-1)
    flat_diagonal = diagonal.reshape(-1)
    plan = jnp.argsort(1 - flat_placed, stable=True)
    active_count = jnp.sum(flat_placed)
    rounds = (active_count + group_size - 1) // group_size

    def advance(round_index, carried):
        row_sums, column_sums = carried
        picked = lax.dynamic_slice_in_dim(plan, round_index * group_size, group_size)
        left_pick = picked // right_count
        right_pick = picked % right_count
        live_flags = jnp.take(flat_placed, picked).astype(jnp.float32)
        mirror_flags = live_flags * (1 - jnp.take(flat_diagonal, picked)).astype(jnp.float32)
        kernel = kernel_tiles(
            left_ctx[left_pick],
            right_ctx[right_pick],
            left_squares[left_pick],
            right_squares[right_pick],
        )
        toward_left, toward_right = tile_terms(
            kernel,
            left_matrix[left_pick],
            right_matrix[right_pick],
            left_onehot[left_pick],
            right_onehot[right_pick],
        )
        row_sums = row_sums.at[left_pick].add(toward_left * live_flags[:, None, None])
        column_sums = column_sums.at[right_pick].add(toward_right * mirror_flags[:, None, None])
        return (row_sums, column_sums)

    start_rows = jnp.zeros((left_count, tile_rows, policies), jnp.float32)
    start_columns = jnp.zeros((right_count, tile_rows, policies), jnp.float32)
    return lax.fori_loop(0, rounds, advance, (start_rows, start_columns))


def on_device(contexts, logged_actions, policy_actions, rewards):
    tile_rows, feature_count = contexts.shape
    left_count = lax.axis_size("col")
    right_count = lax.axis_size("row")
    factor = NACT / (tile_rows * left_count * right_count)
    own_column = lax.axis_index("col")
    own_row = lax.axis_index("row")
    left_ids = jnp.arange(left_count, dtype=jnp.int32)[:, None]
    right_ids = jnp.arange(right_count, dtype=jnp.int32)[None, :]
    first_owner = own_row * left_count + left_ids
    second_owner = right_ids * left_count + own_column
    parity = (first_owner + second_owner) % 2
    placed = jnp.where(
        first_owner == second_owner, 1, jnp.where(first_owner < second_owner, parity, 1 - parity)
    )
    diagonal = ((left_ids == own_column) & (right_ids == own_row)).astype(jnp.int32)
    left_logged, left_policy = (
        lax.all_gather(logged_actions, "col", axis=0, tiled=True),
        lax.all_gather(policy_actions, "col", axis=0, tiled=True),
    )
    right_logged, right_policy = (
        lax.all_gather(logged_actions, "row", axis=0, tiled=True),
        lax.all_gather(policy_actions, "row", axis=0, tiled=True),
    )
    left_onehot = action_features(left_logged, NACT).reshape(left_count, tile_rows, NACT)
    right_onehot = action_features(right_logged, NACT).reshape(right_count, tile_rows, NACT)
    left_first = action_features(left_policy, NACT).reshape(left_count, tile_rows, NPOL * NACT)
    right_first = action_features(right_policy, NACT).reshape(right_count, tile_rows, NPOL * NACT)
    right_ctx = lax.all_gather(contexts, "row", axis=0, tiled=True).reshape(
        right_count, tile_rows, feature_count
    )
    right_squares = jnp.sum(right_ctx.astype(jnp.float32) ** 2, axis=2)
    left_ctx = lax.all_gather(contexts, "col", axis=0, tiled=True).reshape(
        left_count, tile_rows, feature_count
    )
    left_squares = jnp.sum(left_ctx.astype(jnp.float32) ** 2, axis=2)

    def sweep(left_matrix, right_matrix):
        return listed_pass(
            left_ctx,
            left_squares,
            left_matrix,
            left_onehot,
            right_ctx,
            right_squares,
            right_matrix,
            right_onehot,
            placed,
            diagonal,
        )

    def reduce_terms(toward_left, toward_right):
        mine_left = lax.psum_scatter(toward_left, "col", scatter_dimension=0, tiled=True)
        mine_right = lax.psum_scatter(toward_right, "row", scatter_dimension=0, tiled=True)
        return factor * (mine_left[0] + mine_right[0])

    first_left, first_right = sweep(left_first, right_first)
    right_side = reduce_terms(first_left, first_right)
    right_low = right_side.astype(jnp.bfloat16)
    left_rhs = lax.all_gather(right_low, "col", axis=0, tiled=True).reshape(
        left_count, tile_rows, NPOL
    )
    right_rhs = lax.all_gather(right_low, "row", axis=0, tiled=True).reshape(
        right_count, tile_rows, NPOL
    )
    left_second = (left_onehot[:, :, None, :] * left_rhs[:, :, :, None]).reshape(
        left_count, tile_rows, NPOL * NACT
    )
    right_second = (right_onehot[:, :, None, :] * right_rhs[:, :, :, None]).reshape(
        right_count, tile_rows, NPOL * NACT
    )
    second_left, second_right = sweep(left_second, right_second)
    image = reduce_terms(second_left, second_right) + ridge * right_side
    norm_sums, curvature, reward_sums = lax.psum(
        (
            jnp.sum(right_side * right_side, axis=0),
            jnp.sum(right_side * image, axis=0),
            jnp.sum(rewards[:, None] * right_side, axis=0),
        ),
        ("row", "col"),
    )
    alpha = norm_sums / curvature
    weights = alpha[None, :] * right_side
    residual = right_side - alpha[None, :] * image
    values = alpha * reward_sums / (tile_rows * left_count * right_count)
    return (weights, residual, values)


def solution(mesh):
    placed = (
        P(("row", "col"), None),
        P(("row", "col")),
        P(("row", "col"), None),
        P(("row", "col")),
    )
    return jax.shard_map(
        on_device,
        mesh=mesh,
        in_specs=placed,
        out_specs=(P(("row", "col"), None), P(("row", "col"), None), P()),
        check_vma=False,
    )
```

profile of v0, /device:TPU:1, one launch (start us, length us, event | category | flops | bytes accessed | tf_op | source)
XLA Modules:
  0.0 1289.7 jit_solution(7908967299347687956)
XLA Ops:
  11.6 3.2 sort.19
  14.8 29.4 %all-gather.1 = s32[8,1,128]{2,1,0:T(1,128)S(1)} all-gather(s32[1,1,128]{2,1,0:T(1,128)} %bitcast.113), channel_id=1, replica_groups=mesh['row'=8,'col'=32] {'row'}, dimensions={0}, use_global_device_ids=true | all-gather | bytes 4608 | tf_op jit(solution)/shard_map/all_gather | solution.py:126
  44.2 46.1 %all-gather = s32[32,1,128]{2,1,0:T(1,128)S(1)} all-gather(s32[1,1,128]{2,1,0:T(1,128)} %bitcast.114), channel_id=1, replica_groups=mesh['row'=8,'col'=32] {'col'}, dimensions={0}, use_global_device_ids=true | all-gather | bytes 16896 | tf_op jit(solution)/shard_map/all_gather | solution.py:122
  90.3 37.4 %all_gather.26 = s32[1024,8]{0,1:T(8,128)S(1)} all-gather(s32[128,8]{0,1:T(8,128)} %param.12), channel_id=1, replica_groups=mesh['row'=8,'col'=32] {'row'}, dimensions={0}, use_global_device_ids=true | all-gather | bytes 36864 | tf_op jit(solution)/shard_map/all_gather | solution.py:127
  127.8 44.6 %all_gather.28 = s32[4096,8]{0,1:T(8,128)S(1)} all-gather(s32[128,8]{0,1:T(8,128)} %param.12), channel_id=1, replica_groups=mesh['row'=8,'col'=32] {'col'}, dimensions={0}, use_global_device_ids=true | all-gather | bytes 135168 | tf_op jit(solution)/shard_map/all_gather | solution.py:123
  173.5 37.9 %all_gather.25 = bf16[1024,128]{1,0:T(8,128)(2,1)S(1)} all-gather(bf16[128,128]{1,0:T(8,128)(2,1)} %param.10), channel_id=1, replica_groups=mesh['row'=8,'col'=32] {'row'}, dimensions={0}, use_global_device_ids=true | all-gather | bytes 294912 | tf_op jit(solution)/shard_map/all_gather | solution.py:133
  214.6 266.5 %while.32 = (s32[]{:T(128)}, f32[32,128,8]{1,2,0:T(8,128)S(1)}, f32[8,128,8]{1,2,0:T(8,128)S(1)}, s32[]{:T(128)}, s32[256]{0:T(256)}, /*index=5*/bf16[32,128,128...) while((s32[]{:T(128)}, f32[32,128,8]{1,2,0:T(8,128)S(1)}, ...), condition=%wide.region_9.11_spmd.clone.clone, body=%wide.region_4.10_spmd.clone.clone.sunk | while | flops 213377504 | bytes 27038416 | solution.py:102
  217.6 1.9 gather_fusion.1
  222.1 1.9 copy.56
  224.0 9.3 fusion.174
  238.1 2.1 fusion.171
  251.6 1.9 copy.56
  253.6 9.3 fusion.174
  267.7 2.1 fusion.171
  281.2 1.9 copy.56
  283.2 9.3 fusion.174
  297.3 2.1 fusion.171
  310.8 1.9 copy.56
  312.8 9.3 fusion.174
  326.9 2.1 fusion.171
  335.9 1.9 gather_fusion.1
  340.4 1.9 copy.56
  342.3 9.3 fusion.174
  356.5 2.1 fusion.171
  370.0 1.9 copy.56
  371.9 9.3 fusion.174
  386.1 2.1 fusion.171
  395.1 1.9 gather_fusion.1
  399.6 1.9 copy.56
  401.5 9.3 fusion.174
  415.7 2.1 fusion.171
  429.2 1.9 copy.56
  431.1 9.3 fusion.174
  445.3 2.1 fusion.171
  458.8 1.9 copy.56
  460.7 9.3 fusion.174
  474.8 2.1 fusion.171
  484.7 39.5 %all-reduce.1 = f32[8,128,8]{1,2,0:T(8,128)S(1)} all-reduce(f32[8,128,8]{1,2,0:T(8,128)S(1)} %get-tuple-element.391), channel_id=3, replica_groups=mesh['row'=8,'col'=32] {'row'}, use_global_device_ids=true, to_apply=%region_11.13.clone | all-reduce | flops 8192 | bytes 65536
  524.3 203.3 %all-reduce.8.cloned.1.call-done = f32[32,128,8]{1,2,0:T(8,128)} async-done(((f32[32,128,8]{1,2,0:T(8,128)}), f32[32,128,8]{1,2,0:T(8,128)}) %all-reduce.8.cloned.1.call-update) | async-done | bytes 131088
  727.5 2.5 multiply_convert_fusion
  730.1 39.7 %all_gather.31 = bf16[4096,8]{0,1:T(8,128)(2,1)S(1)} all-gather(bf16[128,8]{0,1:T(8,128)(2,1)S(1)} %get-tuple-element.780), channel_id=1, replica_groups=mesh['row'=8,'col'=32] {'col'}, dimensions={0}, use_global_device_ids=true | all-gather | bytes 67584 | tf_op jit(solution)/shard_map/all_gather | solution.py:164
  769.7 35.1 %all_gather.30 = bf16[1024,8]{0,1:T(8,128)(2,1)S(1)} all-gather(bf16[128,8]{0,1:T(8,128)(2,1)S(1)} %get-tuple-element.780), channel_id=1, replica_groups=mesh['row'=8,'col'=32] {'row'}, dimensions={0}, use_global_device_ids=true | all-gather | bytes 18432 | tf_op jit(solution)/shard_map/all_gather | solution.py:167
  804.8 144.6 %while.33 = (s32[]{:T(128)}, f32[32,128,8]{1,2,0:T(8,128)S(1)}, f32[8,128,8]{1,2,0:T(8,128)S(1)}, s32[]{:T(128)}, s32[256]{0:T(256)}, /*index=5*/bf16[32,128,128...) while((s32[]{:T(128)}, f32[32,128,8]{1,2,0:T(8,128)S(1)}, ...), condition=%wide.region_19.21_spmd.clone.clone, body=%wide.region_14.20_spmd.clone.clone.sunk | while | flops 205513184 | bytes 14005563 | solution.py:102
  950.7 45.4 %all-reduce.3 = f32[8,128,8]{1,2,0:T(8,128)S(1)} all-reduce(f32[8,128,8]{1,2,0:T(8,128)S(1)} %get-tuple-element.393), channel_id=5, replica_groups=mesh['row'=8,'col'=32] {'row'}, use_global_device_ids=true, to_apply=%region_21.23.clone | all-reduce | flops 8192 | bytes 65536
  996.1 204.5 %all-reduce.10.cloned.1.call-done = f32[32,128,8]{1,2,0:T(8,128)} async-done(((f32[32,128,8]{1,2,0:T(8,128)}), f32[32,128,8]{1,2,0:T(8,128)}) %all-reduce.10.cloned.1.call-update) | async-done | bytes 131088
  1200.6 2.1 multiply_reduce_fusion.6
  1202.7 77.4 %all-reduce.4 = (f32[8]{0:T(128)S(1)}, f32[8]{0:T(128)S(1)}, f32[8]{0:T(128)S(1)}) all-reduce(f32[8]{0:T(128)S(1)} %get-tuple-element.680, f32[8]{0:T(128)S(1)} %get-tuple-element.679, f32[8]{0:T(128)S(1)} %get-tuple-element.678), channel_id=1, replica_groups=mesh['row'=8,'col'=32] {'row','col'}, use_global_device_ids=true, to_apply=%region_13.15 | all-reduce | flops 24 | bytes 192 | tf_op jit(solution)/shard_map/psum | solution.py:178
  1280.6 2.6 multiply_subtract_fusion
  (896 shorter events, 294.2 us)
Async XLA Ops:
  7.2 205.5 %all-gather.4.cloned.1.call-start = ((), (), s32[]{:S(2)}) async-start(), calls=%async_computation | async-start | bytes 1081344 | tf_op jit(solution)/shard_map/all_gather | solution.py:137
  7.9 719.6 %all-reduce.8.cloned.1.call-start = ((), (), s32[]{:S(2)}) async-start(), calls=%async_computation.1 | async-start | bytes 262144
  217.5 1.9 copy-start.2
  224.0 10.3 copy-start.6
  224.0 10.4 copy-start.8
  240.2 3.0 copy-start.3
  247.1 1.9 copy-start.2
  253.6 10.3 copy-start.6
  253.6 10.4 copy-start.8
  269.8 3.0 copy-start.3
  276.7 1.9 copy-start.2
  283.2 10.3 copy-start.6
  283.2 10.4 copy-start.8
  299.4 3.0 copy-start.3
  306.3 1.9 copy-start.2
  312.8 10.3 copy-start.6
  312.8 10.4 copy-start.8
  329.0 3.0 copy-start.3
  335.9 1.9 copy-start.2
  342.3 10.3 copy-start.6
  342.3 10.4 copy-start.8
  358.6 3.0 copy-start.3
  365.5 1.9 copy-start.2
  371.9 10.3 copy-start.6
  371.9 10.4 copy-start.8
  388.2 3.0 copy-start.3
  395.1 1.9 copy-start.2
  401.5 10.3 copy-start.6
  401.5 10.4 copy-start.8
  417.7 3.0 copy-start.3
  424.7 1.9 copy-start.2
  431.1 10.3 copy-start.6
  431.1 10.4 copy-start.8
  447.3 3.0 copy-start.3
  454.2 1.9 copy-start.2
  460.7 10.3 copy-start.6
  460.7 10.4 copy-start.8
  476.9 3.0 copy-start.3
  481.7 718.9 %all-reduce.10.cloned.1.call-start = ((), (), s32[]{:S(2)}) async-start(), calls=%async_computation.2 | async-start | bytes 262144
  811.9 1.8 copy-start.7
  811.9 1.8 copy-start.9
  843.9 1.8 copy-start.7
  860.0 1.8 copy-start.7
  860.0 1.8 copy-start.9
  892.0 1.8 copy-start.7
  892.1 1.8 copy-start.9
  924.1 1.8 copy-start.7
  924.1 1.8 copy-start.9
  (38 other events, 33.9 us)
Sparse Core Ops, SparseCore 0:
  9.9 63.0 all-gather.3
  481.9 245.6 all-reduce.7
  950.2 250.3 all-reduce.9
where the time goes:
time: 1290 us
  blocking collectives  432 us (33%)
  waiting for transfers between devices  409 us (32%)
  other arithmetic  221 us (17%)
  local copies, waits for them, and re-layouts  183 us (14%)
  matrix products  25.4 us (2%)
  between operations  14.6 us (1%)
    unnamed x5, waiting for transfers between devices  408 us
    convert_element_type x56, other arithmetic, action_features(): jnp.where(levels == 0, constant_term, wave_terms).astype(jnp.bfloat16)  130 us
    unnamed x2, blocking collectives  84.9 us
    psum x1, blocking collectives, on_device(): lax.psum((jnp.sum(right_side * right_side, axis=0), jnp.sum(right_side *...  77.4 us
    all_gather x1, blocking collectives, on_device(): lax.all_gather(logged_actions, 'col', axis=0, tiled=True)  46.1 us
    all_gather x1, blocking collectives, on_device(): lax.all_gather(policy_actions, 'col', axis=0, tiled=True)  44.6 us
    all_gather x1, blocking collectives, on_device(): lax.all_gather(right_low, 'col', axis=0, tiled=True)  39.7 us
    all_gather x1, blocking collectives, on_device(): lax.all_gather(contexts, 'row', axis=0, tiled=True)  37.9 us
  transfers between devices with their start and end apart: 3, of which 2 were waited for; matrix products, arithmetic and copies ran while one was open for 1% of the time, Pallas kernels for 0%

commit v1 on v0

--- a/solution.py
+++ b/solution.py
@@ -1,3 +1,4 @@
+import functools
 import math
 import jax
 import jax.numpy as jnp
@@ -12,6 +13,16 @@
 stride_base = 1009
 phase_step = 0.37
 two_pi = 2.0 * math.pi
+
+
+def clear_pairs_all_for(panel, axis_key, axis_no):
+    return jnp.concatenate(
+        jax.lax.all_to_all(jnp.stack(jax.lax.psum(1, axis_key) * [panel], axis=0), axis_key, 0, 0),
+        axis=axis_no,
+    )
+
+
+spread_shards = functools.partial(clear_pairs_all_for, axis_key="row", axis_no=0)
 
 
 def action_features(chosen, width):
@@ -123,7 +134,7 @@
         lax.all_gather(policy_actions, "col", axis=0, tiled=True),
     )
     right_logged, right_policy = (
-        lax.all_gather(logged_actions, "row", axis=0, tiled=True),
+        spread_shards(logged_actions),
         lax.all_gather(policy_actions, "row", axis=0, tiled=True),
     )
     left_onehot = action_features(left_logged, NACT).reshape(left_count, tile_rows, NACT)

time: 1290 us -> 1280 us (level)
  blocking collectives: 432 us -> 407 us
    all_gather x1 -> x0, blocking collectives: 29.4 us -> none  [on_device(): lax.all_gather(logged_actions, 'row', axis=0, tiled=True)]
  transfers between devices with their start and end apart: 3 -> 4, of which waited for: 2 -> 2; matrix products, arithmetic and copies ran while one was open for 1% -> 1% of each run, Pallas kernels for 0% -> 0%
where the time goes in v1:
time: 1280 us
  waiting for transfers between devices  409 us (32%)
  blocking collectives  407 us (32%)
  other arithmetic  221 us (17%)
  local copies, waits for them, and re-layouts  184 us (14%)
  matrix products  25.5 us (2%)
  between operations  14.6 us (1%)
    unnamed x5, waiting for transfers between devices  409 us
    convert_element_type x56, other arithmetic, action_features(): jnp.where(levels == 0, constant_term, wave_terms).astype(jnp.bfloat16)  130 us
    unnamed x2, blocking collectives  91.4 us
    psum x1, blocking collectives, on_device(): lax.psum((jnp.sum(right_side * right_side, axis=0), jnp.sum(right_side *...  77.3 us
    all_gather x1, blocking collectives, on_device(): lax.all_gather(policy_actions, 'col', axis=0, tiled=True)  44.6 us
    all_gather x1, blocking collectives, on_device(): lax.all_gather(logged_actions, 'col', axis=0, tiled=True)  42.6 us
    all_gather x1, blocking collectives, on_device(): lax.all_gather(right_low, 'col', axis=0, tiled=True)  39.7 us
    all_gather x1, blocking collectives, on_device(): lax.all_gather(contexts, 'row', axis=0, tiled=True)  38.2 us
  transfers between devices with their start and end apart: 4, of which 2 were waited for; matrix products, arithmetic and copies ran while one was open for 1% of the time, Pallas kernels for 0%

profile of v1, /device:TPU:1, one launch (start us, length us, event | category | flops | bytes accessed | tf_op | source)
XLA Modules:
  0.0 1277.8 jit_solution(14978036537835507517)
XLA Ops:
  9.2 11.5 all-to-all-start
  27.0 3.2 sort.19
  30.2 42.6 %all-gather = s32[32,1,128]{2,1,0:T(1,128)S(1)} all-gather(s32[1,1,128]{2,1,0:T(1,128)} %bitcast.113), channel_id=1, replica_groups=mesh['row'=8,'col'=32] {'col'}, dimensions={0}, use_global_device_ids=true | all-gather | bytes 16896 | tf_op jit(solution)/shard_map/all_gather | solution.py:133
  72.8 38.2 %all_gather.23 = s32[1024,8]{0,1:T(8,128)S(1)} all-gather(s32[128,8]{0,1:T(8,128)} %param.12), channel_id=1, replica_groups=mesh['row'=8,'col'=32] {'row'}, dimensions={0}, use_global_device_ids=true | all-gather | bytes 36864 | tf_op jit(solution)/shard_map/all_gather | solution.py:138
  111.1 44.6 %all_gather.25 = s32[4096,8]{0,1:T(8,128)S(1)} all-gather(s32[128,8]{0,1:T(8,128)} %param.12), channel_id=1, replica_groups=mesh['row'=8,'col'=32] {'col'}, dimensions={0}, use_global_device_ids=true | all-gather | bytes 135168 | tf_op jit(solution)/shard_map/all_gather | solution.py:134
  156.7 38.2 %all_gather.22 = bf16[1024,128]{1,0:T(8,128)(2,1)S(1)} all-gather(bf16[128,128]{1,0:T(8,128)(2,1)} %param.10), channel_id=1, replica_groups=mesh['row'=8,'col'=32] {'row'}, dimensions={0}, use_global_device_ids=true | all-gather | bytes 294912 | tf_op jit(solution)/shard_map/all_gather | solution.py:144
  198.1 266.5 %while.32 = (s32[]{:T(128)}, f32[32,128,8]{1,2,0:T(8,128)S(1)}, f32[8,128,8]{1,2,0:T(8,128)S(1)}, s32[]{:T(128)}, s32[256]{0:T(256)}, /*index=5*/bf16[32,128,128...) while((s32[]{:T(128)}, f32[32,128,8]{1,2,0:T(8,128)S(1)}, ...), condition=%wide.region_9.11_spmd.clone.clone, body=%wide.region_4.10_spmd.clone.clone.sunk | while | flops 213377504 | bytes 27038416 | solution.py:113
  201.1 1.9 gather_fusion.1
  205.6 1.9 copy.56
  207.5 9.3 fusion.174
  221.7 2.1 fusion.171
  230.7 1.9 gather_fusion.1
  235.2 1.9 copy.56
  237.1 9.3 fusion.174
  251.3 2.1 fusion.171
  260.3 1.9 gather_fusion.1
  264.8 1.9 copy.56
  266.7 9.3 fusion.174
  280.9 2.1 fusion.171
  294.4 1.9 copy.56
  296.3 9.3 fusion.174
  310.5 2.1 fusion.171
  324.0 1.9 copy.56
  325.9 9.3 fusion.174
  340.1 2.1 fusion.171
  353.6 1.9 copy.56
  355.5 9.3 fusion.174
  369.7 2.1 fusion.171
  383.1 1.9 copy.56
  385.1 9.3 fusion.174
  399.3 2.1 fusion.171
  412.7 1.9 copy.56
  414.7 9.3 fusion.174
  428.8 2.1 fusion.171
  442.3 1.9 copy.56
  444.3 9.3 fusion.174
  458.4 2.1 fusion.171
  465.7 45.9 %all-reduce.1 = f32[8,128,8]{1,2,0:T(8,128)S(1)} all-reduce(f32[8,128,8]{1,2,0:T(8,128)S(1)} %get-tuple-element.391), channel_id=3, replica_groups=mesh['row'=8,'col'=32] {'row'}, use_global_device_ids=true, to_apply=%region_11.13.clone | all-reduce | flops 8192 | bytes 65536
  511.7 204.4 %all-reduce.8.cloned.1.call-done = f32[32,128,8]{1,2,0:T(8,128)} async-done(((f32[32,128,8]{1,2,0:T(8,128)}), f32[32,128,8]{1,2,0:T(8,128)}) %all-reduce.8.cloned.1.call-update) | async-done | bytes 131088
  716.0 2.6 multiply_convert_fusion
  718.6 39.7 %all_gather.27 = bf16[4096,8]{0,1:T(8,128)(2,1)S(1)} all-gather(bf16[128,8]{0,1:T(8,128)(2,1)S(1)} %get-tuple-element.780), channel_id=1, replica_groups=mesh['row'=8,'col'=32] {'col'}, dimensions={0}, use_global_device_ids=true | all-gather | bytes 67584 | tf_op jit(solution)/shard_map/all_gather | solution.py:175
  758.3 35.1 %all_gather.26 = bf16[1024,8]{0,1:T(8,128)(2,1)S(1)} all-gather(bf16[128,8]{0,1:T(8,128)(2,1)S(1)} %get-tuple-element.780), channel_id=1, replica_groups=mesh['row'=8,'col'=32] {'row'}, dimensions={0}, use_global_device_ids=true | all-gather | bytes 18432 | tf_op jit(solution)/shard_map/all_gather | solution.py:178
  793.4 144.1 %while.33 = (s32[]{:T(128)}, f32[32,128,8]{1,2,0:T(8,128)S(1)}, f32[8,128,8]{1,2,0:T(8,128)S(1)}, s32[]{:T(128)}, s32[256]{0:T(256)}, /*index=5*/bf16[32,128,128...) while((s32[]{:T(128)}, f32[32,128,8]{1,2,0:T(8,128)S(1)}, ...), condition=%wide.region_19.21_spmd.clone.clone, body=%wide.region_14.20_spmd.clone.clone.sunk | while | flops 205513184 | bytes 14005563 | solution.py:113
  938.8 45.4 %all-reduce.3 = f32[8,128,8]{1,2,0:T(8,128)S(1)} all-reduce(f32[8,128,8]{1,2,0:T(8,128)S(1)} %get-tuple-element.393), channel_id=5, replica_groups=mesh['row'=8,'col'=32] {'row'}, use_global_device_ids=true, to_apply=%region_21.23.clone | all-reduce | flops 8192 | bytes 65536
  984.2 204.4 %all-reduce.10.cloned.1.call-done = f32[32,128,8]{1,2,0:T(8,128)} async-done(((f32[32,128,8]{1,2,0:T(8,128)}), f32[32,128,8]{1,2,0:T(8,128)}) %all-reduce.10.cloned.1.call-update) | async-done | bytes 131088
  1188.6 2.2 multiply_reduce_fusion.6
  1190.8 77.3 %all-reduce.4 = (f32[8]{0:T(128)S(1)}, f32[8]{0:T(128)S(1)}, f32[8]{0:T(128)S(1)}) all-reduce(f32[8]{0:T(128)S(1)} %get-tuple-element.680, f32[8]{0:T(128)S(1)} %get-tuple-element.679, f32[8]{0:T(128)S(1)} %get-tuple-element.678), channel_id=1, replica_groups=mesh['row'=8,'col'=32] {'row','col'}, use_global_device_ids=true, to_apply=%region_13.15 | all-reduce | flops 24 | bytes 192 | tf_op jit(solution)/shard_map/psum | solution.py:189
  1268.6 2.7 multiply_subtract_fusion
  (898 shorter events, 294.9 us)
Async XLA Ops:
  7.2 189.1 %all-gather.3.cloned.1.call-start = ((), (), s32[]{:S(2)}) async-start(), calls=%async_computation.1 | async-start | bytes 1081344 | tf_op jit(solution)/shard_map/all_gather | solution.py:148
  9.2 189.0 %all-to-all-start = ((s32[8,1,128]{2,1,0:T(1,128)}), s32[8,1,128]{2,1,0:T(1,128)S(1)}, u32[]{:S(2)}, u32[]{:S(2)}) async-start(s32[8,1,128]{2,1,0:T(1,128)} %stack.2), calls=%async_computation | async-start | bytes 8192 | tf_op jit(solution)/shard_map/all_to_all | solution.py:20
  20.6 695.4 %all-reduce.8.cloned.1.call-start = ((), (), s32[]{:S(2)}) async-start(), calls=%async_computation.2 | async-start | bytes 262144
  201.1 1.9 copy-start.2
  207.5 10.4 copy-start.6
  207.5 10.4 copy-start.8
  223.8 3.0 copy-start.3
  230.7 1.9 copy-start.2
  237.1 10.4 copy-start.6
  237.1 10.4 copy-start.8
  253.4 3.0 copy-start.3
  260.3 1.9 copy-start.2
  266.7 10.4 copy-start.6
  266.7 10.4 copy-start.8
  283.0 3.0 copy-start.3
  289.9 1.9 copy-start.2
  296.3 10.4 copy-start.6
  296.3 10.4 copy-start.8
  312.6 3.0 copy-start.3
  319.4 1.9 copy-start.2
  325.9 10.4 copy-start.6
  325.9 10.4 copy-start.8
  342.2 3.0 copy-start.3
  349.0 1.9 copy-start.2
  355.5 10.4 copy-start.6
  355.5 10.4 copy-start.8
  371.7 3.0 copy-start.3
  378.6 1.9 copy-start.2
  385.1 10.4 copy-start.6
  385.1 10.4 copy-start.8
  401.3 3.0 copy-start.3
  408.2 1.9 copy-start.2
  414.7 10.4 copy-start.6
  414.7 10.4 copy-start.8
  430.9 3.0 copy-start.3
  437.8 1.9 copy-start.2
  444.3 10.4 copy-start.6
  444.3 10.4 copy-start.8
  460.5 3.0 copy-start.3
  465.3 723.3 %all-reduce.10.cloned.1.call-start = ((), (), s32[]{:S(2)}) async-start(), calls=%async_computation.3 | async-start | bytes 262144
  800.4 1.7 copy-start.7
  816.4 1.7 copy-start.7
  832.4 1.7 copy-start.7
  848.4 1.7 copy-start.7
  880.3 1.7 copy-start.7
  896.3 1.7 copy-start.7
  912.3 1.7 copy-start.7
  928.3 1.7 copy-start.7
  (39 other events, 36.2 us)
Sparse Core Ops, SparseCore 0:
  9.9 63.8 all-gather.2
  465.5 250.5 all-reduce.7
  938.3 250.2 all-reduce.9
